TPU v7x, 128 devices: a whole 4x4x4 slice. The times are simulated.
128 devices in a mesh: rt: 32 (over x_lo, z, y), mob: 4 (over x_hi, core).
Axes of the slice: x: 4 (x_hi: 2, x_lo: 2; x = x_hi * 2 + x_lo), y: 4, z: 4, core: 2. Of those that a mesh axis runs over, the one named last changes fastest.
Arguments:
- observed: float32 [1024, 64, 1280], P('rt', 'mob'), as said below
- frame_kernel: float32 [31], replicated, may hold values from 0.05 to 1
- scan_kernel: float32 [15], replicated, may hold values from 0.05 to 1
- prec_window: int32 [256], P('rt'), may hold values from 0 to 15
- frag_window: int32 [1024], P('mob'), may hold values from 0 to 15
Outputs:
- estimate: float32 [1024, 64, 1280], P('rt', 'mob')
- correlation: float32 [256, 1024], P('rt', 'mob')
Inputs may be any that keep to these rules, and one draw needn't show every extreme that they name: `observed`: positive intensities.
All inputs are finite; a program needn't handle non-finite values.
Results may differ from a plain program's by a relative error of at most 0.0003.
Values sent between devices are 32-bit elements; how exact they have to be, the bound alone decides.
No kernel may reach another device: no remote copies, remote signals or barrier semaphores. Data moves between devices by JAX's collectives and lax.ppermute only.
A program may use at most 64 MiB of HBM per device.

v0:
```python
import jax
import jax.numpy as jnp
from jax import lax
from jax.sharding import PartitionSpec as P

PREC = 256
ITERS = 2


def extended(cells, sides, width):
    for axis, dim in sides:
        count = lax.axis_size(axis)
        ends = count - 1
        head = lax.slice_in_dim(cells, 0, width, axis=dim)
        tail = lax.slice_in_dim(cells, cells.shape[dim] - width, cells.shape[dim], axis=dim)
        cells = jnp.concatenate(
            [
                lax.ppermute(tail, axis, [(i, (i + 1) % count) for i in range(ends)]),
                cells,
                lax.ppermute(head, axis, [((i + 1) % count, i) for i in range(ends)]),
            ],
            axis=dim,
        )
    return cells


def apply_taps(padded, kernel, along, length):
    running = kernel[0] * lax.slice_in_dim(padded, 0, length, axis=along)
    for tap_index in range(1, kernel.shape[0]):
        running = running + kernel[tap_index] * lax.slice_in_dim(
            padded, tap_index, tap_index + length, axis=along
        )
    return running


def local(observed, frame_kernel, scan_kernel, prec_window, frag_window):
    frames, scan_count, channels = observed.shape
    frame_radius = (frame_kernel.shape[0] - 1) // 2
    scan_radius = (scan_kernel.shape[0] - 1) // 2
    flip_frames = frame_kernel[::-1]
    flip_scans = scan_kernel[::-1]
    estimate = observed
    for iteration in range(ITERS):
        padded_scans = extended(estimate, (("mob", 1),), scan_radius)
        scan_blurred = apply_taps(padded_scans, scan_kernel, 1, scan_count)
        padded_frames = extended(scan_blurred, (("rt", 0),), frame_radius)
        blurred_image = apply_taps(padded_frames, frame_kernel, 0, frames)
        ratio_field = observed / blurred_image
        ratio_frames = extended(ratio_field, (("rt", 0),), frame_radius)
        scan_padded_scans = extended(
            apply_taps(ratio_frames, flip_frames, 0, frames), (("mob", 1),), scan_radius
        )
        estimate = estimate * apply_taps(scan_padded_scans, flip_scans, 1, scan_count)
    profiles = estimate.reshape(frames * scan_count, channels)
    cell_count = frames * scan_count * lax.axis_size("rt") * lax.axis_size("mob")
    channel_total = lax.psum(jnp.sum(profiles, axis=0), ("rt", "mob"))
    channel_mean = channel_total / cell_count
    centered = (profiles - channel_mean).astype(jnp.bfloat16)
    as_float = centered.astype(jnp.float32)
    squares = lax.psum(jnp.sum(as_float * as_float, axis=0), ("rt", "mob"))
    cross_sums = lax.dot_general(
        centered[:, :PREC],
        centered[:, PREC:],
        (((0,), (0,)), ((), ())),
        preferred_element_type=jnp.float32,
    )
    partial_value = lax.psum_scatter(cross_sums, "rt", scatter_dimension=0, tiled=True)
    block_sums = lax.psum_scatter(partial_value, "mob", scatter_dimension=1, tiled=True)
    row_count = prec_window.shape[0]
    column_count = frag_window.shape[0]
    inverse_norm = 1.0 / jnp.sqrt(squares + 1e-06)
    row_inverse = lax.dynamic_slice_in_dim(
        inverse_norm[:PREC], lax.axis_index("rt") * row_count, row_count
    )
    column_inverse = lax.dynamic_slice_in_dim(
        inverse_norm[PREC:], lax.axis_index("mob") * column_count, column_count
    )
    pair_mask = (prec_window[:, None] == frag_window[None, :]).astype(jnp.float32)
    correlation = pair_mask * block_sums * row_inverse[:, None] * column_inverse[None, :]
    return (estimate, correlation)


def solution(mesh):
    placed = (P("rt", "mob", None), P(), P(), P("rt"), P("mob"))
    return jax.shard_map(
        local,
        mesh=mesh,
        in_specs=placed,
        out_specs=(P("rt", "mob", None), P("rt", "mob")),
        check_vma=False,
    )
```

profile of v0, /device:TPU:1, one launch (start us, length us, event | category | flops | bytes accessed | tf_op | source)
XLA Modules:
  0.0 732.5 jit_solution(15922620967570289949)
XLA Ops:
  7.2 1.9 fusion.516
  9.5 6.2 collective-permute-start
  16.0 1.9 collective-permute-start.1
  18.0 0.7 fusion.519
  18.9 9.5 %collective-permute-done = f32[32,7,1280]{2,0,1:T(8,128)S(1)} collective-permute-done((f32[32,7,1280]{2,0,1:T(8,128)S(1)}, f32[32,7,1280]{2,0,1:T(8,128)S(1)}, u32[]{:S(2)}, u32[]{:S(2)}) %collective-permute-start) | collective-permute-done | bytes 1146912 | tf_op jit(solution)/shard_map/ppermute | solution.py:18
  28.4 0.7 copy.17
  29.1 5.6 collective-permute-done.1
  34.7 0.7 copy_dynamic-update-slice_fusion
  35.4 15.1 %fusion.127 = f32[32,16,1280]{2,1,0:T(8,128)S(1)} fusion(f32[32,16,1280]{2,1,0:T(8,128)S(1)} %copy-done, f32[32,7,1280]{2,1,0:T(8,128)S(1)} %copy.17, f32[32,23,1280]{2,1,0:T(8,128)S(1)} %copy_dynamic-update-slice_fusion, f32[]{:T(128)} %bitcast.16, f32[]{:T(128)} %bitcast.15, f32[]{:T(128)} %bitcast.14, f32[]{:T(128)} %bitcast.13, f32[]{:T(128)} %bitcast.12, ...), kind=kLoop, calls=%fused_computation.435 | loop fusion | flops 23592960 | bytes 24739900 | tf_op jit(solution)/shard_map/add | solution.py:30
  50.7 3.3 collective-permute-start.2
  53.9 1.3 collective-permute-start.3
  55.3 0.7 fusion.518
  55.9 0.7 fusion.517
  56.7 10.9 %collective-permute-done.2 = f32[15,16,1280]{2,1,0:T(8,128)S(1)} collective-permute-done((f32[15,16,1280]{2,1,0:T(8,128)S(1)}, f32[15,16,1280]{2,1,0:T(8,128)S(1)}, u32[]{:S(2)}, u32[]{:S(2)}) %collective-permute-start.2) | collective-permute-done | bytes 1228832 | tf_op jit(solution)/shard_map/ppermute | solution.py:18
  67.5 3.9 collective-permute-done.3
  71.4 1.1 copy-done.5
  72.5 34.5 %fusion.405 = f32[32,16,1280]{2,1,0:T(8,128)} fusion(f32[32,16,1280]{2,1,0:T(8,128)S(1)} %copy-done, f32[32,16,1280]{2,1,0:T(8,128)S(1)} %fusion.127, f32[15,16,1280]{2,1,0:T(8,128)} %copy-done.5, f32[15,16,1280]{2,1,0:T(8,128)S(1)} %collective-permute-done.2, f32[]{:T(128)} %bitcast.45, f32[]{:T(128)} %bitcast.44, f32[]{:T(128)} %bitcast.43, f32[]{:T(128)} %bitcast.42, ...), kind=kLoop, calls=%fused_computation.713 | loop fusion | flops 60293120 | bytes 10322044 | tf_op jit(solution)/shard_map/div | solution.py:48
  107.0 1.8 fusion.514
  108.8 3.2 collective-permute-start.4
  112.0 1.3 collective-permute-start.5
  113.3 13.4 %collective-permute-done.4 = f32[15,16,1280]{2,1,0:T(8,128)S(1)} collective-permute-done((f32[15,16,1280]{2,1,0:T(8,128)S(1)}, f32[15,16,1280]{2,1,0:T(8,128)S(1)}, u32[]{:S(2)}, u32[]{:S(2)}) %collective-permute-start.4) | collective-permute-done | bytes 1228832 | tf_op jit(solution)/shard_map/ppermute | solution.py:18
  126.7 4.3 collective-permute-done.5
  130.9 53.8 %fusion.318 = f32[32,16,1280]{2,1,0:T(8,128)S(1)} fusion(f32[32,16,1280]{2,1,0:T(8,128)} %fusion.405, f32[15,16,1280]{2,1,0:T(8,128)} %collective-permute-done.5, f32[15,16,1280]{2,1,0:T(8,128)S(1)} %collective-permute-done.4, f32[]{:T(128)} %bitcast.45, f32[]{:T(128)} %bitcast.44, f32[]{:T(128)} %bitcast.43, f32[]{:T(128)} %bitcast.42, f32[]{:T(128)} %bitcast.41, ...), kind=kLoop, calls=%fused_computation.626 | loop fusion | flops 59637760 | bytes 7700604 | tf_op jit(solution)/shard_map/add | solution.py:30
  185.0 1.3 copy-done.2
  186.6 3.4 collective-permute-start.6
  190.4 2.2 collective-permute-start.7
  192.6 10.0 %collective-permute-done.6 = f32[32,7,1280]{2,0,1:T(8,128)S(1)} collective-permute-done((f32[32,7,1280]{2,0,1:T(8,128)S(1)}, f32[32,7,1280]{2,0,1:T(8,128)S(1)}, u32[]{:S(2)}, u32[]{:S(2)}) %collective-permute-start.6) | collective-permute-done | bytes 1146912 | tf_op jit(solution)/shard_map/ppermute | solution.py:18
  202.6 0.7 copy.21
  203.3 6.1 collective-permute-done.7
  209.4 0.7 copy.23
  210.0 16.5 %fusion.81 = f32[32,16,1280]{2,1,0:T(8,128)S(1)} fusion(f32[32,16,1280]{2,1,0:T(8,128)S(1)} %copy-done, f32[32,16,1280]{2,1,0:T(8,128)S(1)} %copy-done.3, f32[32,7,1280]{2,1,0:T(8,128)S(1)} %copy.23, f32[32,7,1280]{2,1,0:T(8,128)S(1)} %copy.21, f32[]{:T(128)} %bitcast.16, f32[]{:T(128)} %bitcast.15, f32[]{:T(128)} %bitcast.14, f32[]{:T(128)} %bitcast.13, ...), kind=kLoop, calls=%fused_computation.389 | loop fusion | flops 28835840 | bytes 10158140 | tf_op jit(solution)/shard_map/mul | solution.py:53
  227.2 1.9 collective-permute-start.8
  229.5 2.5 collective-permute-start.9
  231.9 9.9 %collective-permute-done.8 = f32[32,7,1280]{2,0,1:T(8,128)S(1)} collective-permute-done((f32[32,7,1280]{2,0,1:T(8,128)S(1)}, f32[32,7,1280]{2,0,1:T(8,128)S(1)}, u32[]{:S(2)}, u32[]{:S(2)}) %collective-permute-start.8) | collective-permute-done | bytes 1146912 | tf_op jit(solution)/shard_map/ppermute | solution.py:18
  241.9 0.7 copy.25
  242.5 5.6 collective-permute-done.9
  248.1 0.7 copy.27
  248.8 16.3 %fusion.42 = f32[32,16,1280]{2,1,0:T(8,128)S(1)} fusion(f32[32,16,1280]{2,1,0:T(8,128)S(1)} %fusion.81, f32[32,7,1280]{2,1,0:T(8,128)S(1)} %copy.27, f32[32,7,1280]{2,1,0:T(8,128)S(1)} %copy.25, f32[]{:T(128)} %bitcast.16, f32[]{:T(128)} %bitcast.15, f32[]{:T(128)} %bitcast.14, f32[]{:T(128)} %bitcast.13, f32[]{:T(128)} %bitcast.12, f32[]{:T(128)} %bitcast.11, ...), kind=kLoop, calls=%fused_computation.350 | loop fusion | flops 28180480 | bytes 7536700 | tf_op jit(solution)/shard_map/add | solution.py:30
  265.1 1.5 copy-done.4
  266.8 4.6 collective-permute-start.10
  271.4 1.3 collective-permute-start.11
  272.7 12.5 %collective-permute-done.10 = f32[15,16,1280]{2,1,0:T(8,128)S(1)} collective-permute-done((f32[15,16,1280]{2,1,0:T(8,128)S(1)}, f32[15,16,1280]{2,1,0:T(8,128)S(1)}, u32[]{:S(2)}, u32[]{:S(2)}) %collective-permute-start.10) | collective-permute-done | bytes 1228832 | tf_op jit(solution)/shard_map/ppermute | solution.py:18
  285.2 4.3 collective-permute-done.11
  289.4 54.3 %fusion.232 = f32[32,16,1280]{2,1,0:T(8,128)} fusion(f32[32,16,1280]{2,1,0:T(8,128)S(1)} %copy-done, f32[32,16,1280]{2,1,0:T(8,128)} %copy-done.4, f32[15,16,1280]{2,1,0:T(8,128)} %collective-permute-done.11, f32[15,16,1280]{2,1,0:T(8,128)S(1)} %collective-permute-done.10, f32[]{:T(128)} %bitcast.45, f32[]{:T(128)} %bitcast.44, f32[]{:T(128)} %bitcast.43, ...), kind=kLoop, calls=%fused_computation.540 | loop fusion | flops 60293120 | bytes 10322044 | tf_op jit(solution)/shard_map/div | solution.py:48
  343.7 1.8 fusion.510
  345.6 3.8 collective-permute-start.12
  349.3 1.5 collective-permute-start.13
  350.8 13.4 %collective-permute-done.12 = f32[15,16,1280]{2,1,0:T(8,128)S(1)} collective-permute-done((f32[15,16,1280]{2,1,0:T(8,128)S(1)}, f32[15,16,1280]{2,1,0:T(8,128)S(1)}, u32[]{:S(2)}, u32[]{:S(2)}) %collective-permute-start.12) | collective-permute-done | bytes 1228832 | tf_op jit(solution)/shard_map/ppermute | solution.py:18
  364.3 4.5 collective-permute-done.13
  368.8 52.5 %fusion.145 = f32[32,16,1280]{2,1,0:T(8,128)S(1)} fusion(f32[32,16,1280]{2,1,0:T(8,128)} %fusion.232, f32[15,16,1280]{2,1,0:T(8,128)} %collective-permute-done.13, f32[15,16,1280]{2,1,0:T(8,128)S(1)} %collective-permute-done.12, f32[]{:T(128)} %bitcast.45, f32[]{:T(128)} %bitcast.44, f32[]{:T(128)} %bitcast.43, f32[]{:T(128)} %bitcast.42, f32[]{:T(128)} %bitcast.41, ...), kind=kLoop, calls=%fused_computation.453 | loop fusion | flops 59637760 | bytes 7700604 | tf_op jit(solution)/shard_map/add | solution.py:30
  421.9 2.3 collective-permute-start.14
  424.6 2.1 collective-permute-start.15
  426.7 10.3 %collective-permute-done.14 = f32[32,7,1280]{2,0,1:T(8,128)S(1)} collective-permute-done((f32[32,7,1280]{2,0,1:T(8,128)S(1)}, f32[32,7,1280]{2,0,1:T(8,128)S(1)}, u32[]{:S(2)}, u32[]{:S(2)}) %collective-permute-start.14) | collective-permute-done | bytes 1146912 | tf_op jit(solution)/shard_map/ppermute | solution.py:18
  437.0 0.7 copy.29
  437.6 5.6 collective-permute-done.15
  443.2 0.7 copy.31
  443.9 17.4 %fusion.507 = (f32[1280]{0:T(1024)S(1)}, f32[32,16,1280]{2,1,0:T(8,128)}) fusion(f32[32,16,1280]{2,1,0:T(8,128)S(1)} %fusion.81, f32[32,7,1280]{2,1,0:T(8,128)S(1)} %copy.31, f32[32,16,1280]{2,1,0:T(8,128)S(1)} %fusion.145, f32[]{:T(128)} %bitcast.3, f32[]{:T(128)} %bitcast.4, f32[]{:T(128)} %bitcast.5, f32[]{:T(128)} %bitcast.6, f32[]{:T(128)} %bitcast.7, ...), kind=kLoop, calls=%fused_computation.845 | loop fusion | flops 29489920 | bytes 10163260 | tf_op jit(solution)/shard_map/reduce_sum | solution.py:56
  461.3 74.5 %psum.14 = f32[1280]{0:T(1024)S(1)} all-reduce(f32[1280]{0:T(1024)S(1)} %get-tuple-element.4), channel_id=1, replica_groups=mesh['rt'=32,'mob'=4] {'rt','mob'}, use_global_device_ids=true, to_apply=%region_1.0 | all-reduce | flops 1280 | bytes 10240 | tf_op jit(solution)/shard_map/psum | solution.py:56
  535.9 1.9 fusion.503
  537.8 1.5 fusion.504
  540.2 64.9 %psum.15 = f32[1280]{0:T(1024)S(1)} all-reduce(f32[1280]{0:T(1024)S(1)} %multiply_reduce_fusion), channel_id=1, replica_groups=mesh['rt'=32,'mob'=4] {'rt','mob'}, use_global_device_ids=true, to_apply=%region_5.0 | all-reduce | flops 1280 | bytes 10240 | tf_op jit(solution)/shard_map/psum | solution.py:60
  605.2 69.0 %reduce-scatter.3.cloned.1.call-done = f32[8,1024]{1,0:T(8,128)} async-done(((f32[256,1024]{1,0:T(8,128)}), f32[8,1024]{1,0:T(8,128)}) %reduce-scatter.3.cloned.1.call-update) | async-done | bytes 32784 | tf_op jit(solution)/shard_map/reduce_scatter | solution.py:67
  674.4 49.9 %reduce-scatter.5.cloned.1.call-done = f32[8,256]{1,0:T(8,128)} async-done(((f32[8,1024]{1,0:T(8,128)}), f32[8,256]{1,0:T(8,128)}) %reduce-scatter.5.cloned.1.call-update) | async-done | bytes 8208 | tf_op jit(solution)/shard_map/reduce_scatter | solution.py:68
  724.3 1.4 multiply_multiply_fusion
  (42 shorter events, 5.3 us)
Async XLA Ops:
  7.2 667.0 %reduce-scatter.3.cloned.1.call-start = ((), (), s32[]{:S(2)}) async-start(), calls=%async_computation.2 | async-start | bytes 1081344 | tf_op jit(solution)/shard_map/reduce_scatter | solution.py:67
  9.1 8.9 %copy-start.7 = (f32[15]{0:T(128)S(1)}, f32[15]{0:T(128)}, u32[]{:S(2)}) copy-start(f32[15]{0:T(128)} %param.7) | copy-start | bytes 184
  9.1 9.6 %copy-start = (f32[32,16,1280]{2,1,0:T(8,128)S(1)}, f32[32,16,1280]{2,1,0:T(8,128)}, u32[]{:S(2)}) copy-start(f32[32,16,1280]{2,1,0:T(8,128)} %param.5) | copy-start | bytes 7864324
  9.5 18.9 %collective-permute-start = (f32[32,7,1280]{2,0,1:T(8,128)S(1)}, f32[32,7,1280]{2,0,1:T(8,128)S(1)}, u32[]{:S(2)}, u32[]{:S(2)}) collective-permute-start(f32[32,7,1280]{2,0,1:T(8,128)S(1)} %copy.32), channel_id=1, source_target_pairs={{0,1},{1,2},{2,3},{4,5},{5,6},{6,7},{8,9},{9,10},{10,11},{12,13},{... | collective-permute-start | bytes 3440648 | tf_op jit(solution)/shard_map/ppermute | solution.py:18
  16.0 18.7 %collective-permute-start.1 = (f32[32,7,1280]{2,0,1:T(8,128)S(1)}, f32[32,7,1280]{2,0,1:T(8,128)S(1)}, u32[]{:S(2)}, u32[]{:S(2)}) collective-permute-start(f32[32,7,1280]{2,0,1:T(8,128)S(1)} %copy.33), channel_id=1, source_target_pairs={{1,0},{2,1},{3,2},{5,4},{6,5},{7,6},{9,8},{10,9},{11,10},{13,12},{... | collective-permute-start | bytes 3440648 | tf_op jit(solution)/shard_map/ppermute | solution.py:20
  50.5 4.8 copy-start.6
  50.7 16.9 %collective-permute-start.2 = (f32[15,16,1280]{2,1,0:T(8,128)S(1)}, f32[15,16,1280]{2,1,0:T(8,128)S(1)}, u32[]{:S(2)}, u32[]{:S(2)}) collective-permute-start(f32[15,16,1280]{2,1,0:T(8,128)S(1)} %get-tuple-element.18), channel_id=1, source_target_pairs={{0,4},{4,8},{8,12},{12,16},{16,20},{20,24},{24,28},{28,32},{32,36}... | collective-permute-start | bytes 3686408 | tf_op jit(solution)/shard_map/ppermute | solution.py:18
  53.9 17.5 %collective-permute-start.3 = (f32[15,16,1280]{2,1,0:T(8,128)S(1)}, f32[15,16,1280]{2,1,0:T(8,128)S(1)}, u32[]{:S(2)}, u32[]{:S(2)}) collective-permute-start(f32[15,16,1280]{2,1,0:T(8,128)S(1)} %get-tuple-element.19), channel_id=1, source_target_pairs={{4,0},{8,4},{12,8},{16,12},{20,16},{24,20},{28,24},{32,28},{36,32}... | collective-permute-start | bytes 3686408 | tf_op jit(solution)/shard_map/ppermute | solution.py:20
  71.4 1.1 copy-start.5
  108.8 17.9 %collective-permute-start.4 = (f32[15,16,1280]{2,1,0:T(8,128)S(1)}, f32[15,16,1280]{2,1,0:T(8,128)S(1)}, u32[]{:S(2)}, u32[]{:S(2)}) collective-permute-start(f32[15,16,1280]{2,1,0:T(8,128)S(1)} %get-tuple-element.16), channel_id=1, source_target_pairs={{0,4},{4,8},{8,12},{12,16},{16,20},{20,24},{24,28},{28,32},{32,36}... | collective-permute-start | bytes 3686408 | tf_op jit(solution)/shard_map/ppermute | solution.py:18
  112.0 18.9 %collective-permute-start.5 = (f32[15,16,1280]{2,1,0:T(8,128)S(1)}, f32[15,16,1280]{2,1,0:T(8,128)}, u32[]{:S(2)}, u32[]{:S(2)}) collective-permute-start(f32[15,16,1280]{2,1,0:T(8,128)S(1)} %get-tuple-element.17), channel_id=1, source_target_pairs={{4,0},{8,4},{12,8},{16,12},{20,16},{24,20},{28,24},{32,28},{36,32}... | collective-permute-start | bytes 3686408 | tf_op jit(solution)/shard_map/ppermute | solution.py:20
  184.7 1.5 copy-start.2
  186.6 16.0 %collective-permute-start.6 = (f32[32,7,1280]{2,0,1:T(8,128)S(1)}, f32[32,7,1280]{2,0,1:T(8,128)S(1)}, u32[]{:S(2)}, u32[]{:S(2)}) collective-permute-start(f32[32,7,1280]{2,0,1:T(8,128)S(1)} %copy.20), channel_id=1, source_target_pairs={{0,1},{1,2},{2,3},{4,5},{5,6},{6,7},{8,9},{9,10},{10,11},{12,13},{... | collective-permute-start | bytes 3440648 | tf_op jit(solution)/shard_map/ppermute | solution.py:18
  190.4 19.6 %copy-start.3 = (f32[32,16,1280]{2,1,0:T(8,128)S(1)}, f32[32,16,1280]{2,1,0:T(8,128)}, u32[]{:S(2)}) copy-start(f32[32,16,1280]{2,1,0:T(8,128)} %copy-done.2) | copy-start | bytes 7864324
  190.4 18.9 %collective-permute-start.7 = (f32[32,7,1280]{2,0,1:T(8,128)S(1)}, f32[32,7,1280]{2,0,1:T(8,128)S(1)}, u32[]{:S(2)}, u32[]{:S(2)}) collective-permute-start(f32[32,7,1280]{2,0,1:T(8,128)S(1)} %copy.22), channel_id=1, source_target_pairs={{1,0},{2,1},{3,2},{5,4},{6,5},{7,6},{9,8},{10,9},{11,10},{13,12},{... | collective-permute-start | bytes 3440648 | tf_op jit(solution)/shard_map/ppermute | solution.py:20
  227.2 14.7 %collective-permute-start.8 = (f32[32,7,1280]{2,0,1:T(8,128)S(1)}, f32[32,7,1280]{2,0,1:T(8,128)S(1)}, u32[]{:S(2)}, u32[]{:S(2)}) collective-permute-start(f32[32,7,1280]{2,0,1:T(8,128)S(1)} %copy.24), channel_id=1, source_target_pairs={{0,1},{1,2},{2,3},{4,5},{5,6},{6,7},{8,9},{9,10},{10,11},{12,13},{... | collective-permute-start | bytes 3440648 | tf_op jit(solution)/shard_map/ppermute | solution.py:18
  229.5 18.7 %collective-permute-start.9 = (f32[32,7,1280]{2,0,1:T(8,128)S(1)}, f32[32,7,1280]{2,0,1:T(8,128)S(1)}, u32[]{:S(2)}, u32[]{:S(2)}) collective-permute-start(f32[32,7,1280]{2,0,1:T(8,128)S(1)} %copy.26), channel_id=1, source_target_pairs={{1,0},{2,1},{3,2},{5,4},{6,5},{7,6},{9,8},{10,9},{11,10},{13,12},{... | collective-permute-start | bytes 3440648 | tf_op jit(solution)/shard_map/ppermute | solution.py:20
  265.1 1.5 copy-start.4
  266.8 18.4 %collective-permute-start.10 = (f32[15,16,1280]{2,1,0:T(8,128)S(1)}, f32[15,16,1280]{2,1,0:T(8,128)S(1)}, u32[]{:S(2)}, u32[]{:S(2)}) collective-permute-start(f32[15,16,1280]{2,1,0:T(8,128)S(1)} %get-tuple-element.10), channel_id=1, source_target_pairs={{0,4},{4,8},{8,12},{12,16},{16,20},{20,24},{24,28},{28,32},{32,36}... | collective-permute-start | bytes 3686408 | tf_op jit(solution)/shard_map/ppermute | solution.py:18
  271.4 18.1 %collective-permute-start.11 = (f32[15,16,1280]{2,1,0:T(8,128)S(1)}, f32[15,16,1280]{2,1,0:T(8,128)}, u32[]{:S(2)}, u32[]{:S(2)}) collective-permute-start(f32[15,16,1280]{2,1,0:T(8,128)S(1)} %get-tuple-element.11), channel_id=1, source_target_pairs={{4,0},{8,4},{12,8},{16,12},{20,16},{24,20},{28,24},{32,28},{36,32}... | collective-permute-start | bytes 3686408 | tf_op jit(solution)/shard_map/ppermute | solution.py:20
  345.6 18.7 %collective-permute-start.12 = (f32[15,16,1280]{2,1,0:T(8,128)S(1)}, f32[15,16,1280]{2,1,0:T(8,128)S(1)}, u32[]{:S(2)}, u32[]{:S(2)}) collective-permute-start(f32[15,16,1280]{2,1,0:T(8,128)S(1)} %get-tuple-element.8), channel_id=1, source_target_pairs={{0,4},{4,8},{8,12},{12,16},{16,20},{20,24},{24,28},{28,32},{32,36}... | collective-permute-start | bytes 3686408 | tf_op jit(solution)/shard_map/ppermute | solution.py:18
  349.3 19.4 %collective-permute-start.13 = (f32[15,16,1280]{2,1,0:T(8,128)S(1)}, f32[15,16,1280]{2,1,0:T(8,128)}, u32[]{:S(2)}, u32[]{:S(2)}) collective-permute-start(f32[15,16,1280]{2,1,0:T(8,128)S(1)} %get-tuple-element.9), channel_id=1, source_target_pairs={{4,0},{8,4},{12,8},{16,12},{20,16},{24,20},{28,24},{32,28},{36,32}... | collective-permute-start | bytes 3686408 | tf_op jit(solution)/shard_map/ppermute | solution.py:20
  421.9 15.1 %collective-permute-start.14 = (f32[32,7,1280]{2,0,1:T(8,128)S(1)}, f32[32,7,1280]{2,0,1:T(8,128)S(1)}, u32[]{:S(2)}, u32[]{:S(2)}) collective-permute-start(f32[32,7,1280]{2,0,1:T(8,128)S(1)} %copy.28), channel_id=1, source_target_pairs={{0,1},{1,2},{2,3},{4,5},{5,6},{6,7},{8,9},{9,10},{10,11},{12,13},{... | collective-permute-start | bytes 3440648 | tf_op jit(solution)/shard_map/ppermute | solution.py:18
  424.6 18.7 %collective-permute-start.15 = (f32[32,7,1280]{2,0,1:T(8,128)S(1)}, f32[32,7,1280]{2,0,1:T(8,128)S(1)}, u32[]{:S(2)}, u32[]{:S(2)}) collective-permute-start(f32[32,7,1280]{2,0,1:T(8,128)S(1)} %copy.30), channel_id=1, source_target_pairs={{1,0},{2,1},{3,2},{5,4},{6,5},{7,6},{9,8},{10,9},{11,10},{13,12},{... | collective-permute-start | bytes 3440648 | tf_op jit(solution)/shard_map/ppermute | solution.py:20
  537.8 2.1 copy-start.1
  537.8 186.5 %copy-start.8 = (s32[256]{0:T(256)S(1)}, s32[256]{0:T(256)}, u32[]{:S(2)}) copy-start(s32[256]{0:T(256)} %param.9) | copy-start | bytes 3076
  537.8 186.5 %copy-start.9 = (s32[8]{0:T(128)S(1)}, s32[8]{0:T(128)}, u32[]{:S(2)}) copy-start(s32[8]{0:T(128)} %param.8) | copy-start | bytes 100
  539.3 185.0 %reduce-scatter.5.cloned.1.call-start = ((), (), s32[]{:S(2)}) async-start(), calls=%async_computation.3 | async-start | bytes 40960 | tf_op jit(solution)/shard_map/reduce_scatter | solution.py:68
Sparse Core Ops, SparseCore 0:
  539.4 134.6 reduce-scatter.2
  676.6 47.5 reduce-scatter.4
where the time goes:
time: 735 us; the launch traced here: 733 us
  other arithmetic  264 us (36%)
  waiting for transfers between devices  249 us (34%)
  blocking collectives  139 us (19%)
  starting transfers between devices  42.8 us (6%)
  local copies, waits for them, and re-layouts  21.7 us (3%)
  between operations  14.5 us (2%)
    add x4, other arithmetic, apply_taps(): running + kernel[tap_index] * lax.slice_in_dim(padded, tap_index, tap_ind...  138 us
    ppermute x8, waiting for transfers between devices, extended(): lax.ppermute(tail, axis, [(i, (i + 1) % count) for i in range(ends)])  89.9 us
    div x2, other arithmetic, local(): ratio_field = observed / blurred_image  88.8 us
    psum x1, blocking collectives, local(): channel_total = lax.psum(jnp.sum(profiles, axis=0), ('rt', 'mob'))  74.5 us
    reduce_scatter x1, waiting for transfers between devices, local(): lax.psum_scatter(cross_sums, 'rt', scatter_dimension=0, tiled=True)  69 us
    psum x1, blocking collectives, local(): squares = lax.psum(jnp.sum(as_float * as_float, axis=0), ('rt', 'mob'))  64.9 us
    reduce_scatter x1, waiting for transfers between devices, local(): lax.psum_scatter(partial_value, 'mob', scatter_dimension=1, tiled=True)  49.9 us
    ppermute x8, waiting for transfers between devices, extended(): lax.ppermute(head, axis, [((i + 1) % count, i) for i in range(ends)])  39.8 us
  transfers between devices with their start and end apart: 18, of which 18 were waited for; matrix products, arithmetic and copies ran while one was open for 1% of the time, Pallas kernels for 0%

commit v1 on v0

--- a/solution.py
+++ b/solution.py
@@ -53,7 +53,7 @@
         estimate = estimate * apply_taps(scan_padded_scans, flip_scans, 1, scan_count)
     profiles = estimate.reshape(frames * scan_count, channels)
     cell_count = frames * scan_count * lax.axis_size("rt") * lax.axis_size("mob")
-    channel_total = lax.psum(jnp.sum(profiles, axis=0), ("rt", "mob"))
+    channel_total = lax.psum(lax.psum(jnp.sum(profiles, axis=0), "mob"), "rt")
     channel_mean = channel_total / cell_count
     centered = (profiles - channel_mean).astype(jnp.bfloat16)
     as_float = centered.astype(jnp.float32)

time: 735 us -> 759 us (1.033)
  blocking collectives: 139 us -> 164 us
    psum x1, blocking collectives: 64.9 us -> 91.1 us  [local(): squares = lax.psum(jnp.sum(as_float * as_float, axis=0), ('rt', 'mob'))]
    psum x1 -> x2, blocking collectives: 74.5 us -> 72.6 us  [local(): channel_total = lax.psum(lax.psum(jnp.sum(profiles, axis=0), 'mob'), 'rt')]
where the time goes in v1:
time: 759 us; the launch traced here: 757 us
  other arithmetic  264 us (35%)
  waiting for transfers between devices  249 us (33%)
  blocking collectives  164 us (22%)
  starting transfers between devices  42.8 us (6%)
  local copies, waits for them, and re-layouts  21.9 us (3%)
  between operations  14.5 us (2%)
    add x4, other arithmetic, apply_taps(): running + kernel[tap_index] * lax.slice_in_dim(padded, tap_index, tap_ind...  137 us
    psum x1, blocking collectives, local(): squares = lax.psum(jnp.sum(as_float * as_float, axis=0), ('rt', 'mob'))  91.1 us
    ppermute x8, waiting for transfers between devices, extended(): lax.ppermute(tail, axis, [(i, (i + 1) % count) for i in range(ends)])  89.9 us
    div x2, other arithmetic, local(): ratio_field = observed / blurred_image  89.1 us
    psum x2, blocking collectives, local(): channel_total = lax.psum(lax.psum(jnp.sum(profiles, axis=0), 'mob'), 'rt')  72.6 us
    reduce_scatter x1, waiting for transfers between devices, local(): lax.psum_scatter(cross_sums, 'rt', scatter_dimension=0, tiled=True)  70 us
    reduce_scatter x1, waiting for transfers between devices, local(): lax.psum_scatter(partial_value, 'mob', scatter_dimension=1, tiled=True)  49.3 us
    ppermute x8, waiting for transfers between devices, extended(): lax.ppermute(head, axis, [((i + 1) % count, i) for i in range(ends)])  39.8 us
  transfers between devices with their start and end apart: 18, of which 18 were waited for; matrix products, arithmetic and copies ran while one was open for 1% of the time, Pallas kernels for 0%

profile of v1, /device:TPU:1, one launch (start us, length us, event | category | flops | bytes accessed | tf_op | source)
XLA Modules:
  0.0 756.8 jit_solution(2931115726858465187)
XLA Ops:
  7.2 1.9 fusion.516
  9.5 6.2 collective-permute-start
  16.0 1.9 collective-permute-start.1
  18.0 0.7 fusion.519
  18.9 9.6 %collective-permute-done = f32[32,7,1280]{2,0,1:T(8,128)S(1)} collective-permute-done((f32[32,7,1280]{2,0,1:T(8,128)S(1)}, f32[32,7,1280]{2,0,1:T(8,128)S(1)}, u32[]{:S(2)}, u32[]{:S(2)}) %collective-permute-start) | collective-permute-done | bytes 1146912 | tf_op jit(solution)/shard_map/ppermute | solution.py:18
  28.4 0.7 copy.17
  29.1 5.6 collective-permute-done.1
  35.4 15.0 %fusion.127 = f32[32,16,1280]{2,1,0:T(8,128)S(1)} fusion(f32[32,16,1280]{2,1,0:T(8,128)S(1)} %copy-done, f32[32,7,1280]{2,1,0:T(8,128)S(1)} %copy.17, f32[32,23,1280]{2,1,0:T(8,128)S(1)} %copy_dynamic-update-slice_fusion, f32[]{:T(128)} %bitcast.16, f32[]{:T(128)} %bitcast.15, f32[]{:T(128)} %bitcast.14, f32[]{:T(128)} %bitcast.13, f32[]{:T(128)} %bitcast.12, ...), kind=kLoop, calls=%fused_computation.435 | loop fusion | flops 23592960 | bytes 24739900 | tf_op jit(solution)/shard_map/add | solution.py:30
  50.6 3.3 collective-permute-start.2
  53.9 1.3 collective-permute-start.3
  55.2 0.7 fusion.518
  55.9 0.7 fusion.517
  56.6 10.9 %collective-permute-done.2 = f32[15,16,1280]{2,1,0:T(8,128)S(1)} collective-permute-done((f32[15,16,1280]{2,1,0:T(8,128)S(1)}, f32[15,16,1280]{2,1,0:T(8,128)S(1)}, u32[]{:S(2)}, u32[]{:S(2)}) %collective-permute-start.2) | collective-permute-done | bytes 1228832 | tf_op jit(solution)/shard_map/ppermute | solution.py:18
  67.5 3.9 collective-permute-done.3
  71.4 1.1 copy-done.4
  72.4 34.4 %fusion.405 = f32[32,16,1280]{2,1,0:T(8,128)} fusion(f32[32,16,1280]{2,1,0:T(8,128)S(1)} %copy-done, f32[32,16,1280]{2,1,0:T(8,128)S(1)} %fusion.127, f32[15,16,1280]{2,1,0:T(8,128)} %copy-done.4, f32[15,16,1280]{2,1,0:T(8,128)S(1)} %collective-permute-done.2, f32[]{:T(128)} %bitcast.45, f32[]{:T(128)} %bitcast.44, f32[]{:T(128)} %bitcast.43, f32[]{:T(128)} %bitcast.42, ...), kind=kLoop, calls=%fused_computation.713 | loop fusion | flops 60293120 | bytes 10322044 | tf_op jit(solution)/shard_map/div | solution.py:48
  106.9 1.8 fusion.514
  108.7 3.2 collective-permute-start.4
  111.9 1.3 collective-permute-start.5
  113.2 13.4 %collective-permute-done.4 = f32[15,16,1280]{2,1,0:T(8,128)S(1)} collective-permute-done((f32[15,16,1280]{2,1,0:T(8,128)S(1)}, f32[15,16,1280]{2,1,0:T(8,128)S(1)}, u32[]{:S(2)}, u32[]{:S(2)}) %collective-permute-start.4) | collective-permute-done | bytes 1228832 | tf_op jit(solution)/shard_map/ppermute | solution.py:18
  126.6 4.3 collective-permute-done.5
  130.9 52.8 %fusion.318 = f32[32,16,1280]{2,1,0:T(8,128)S(1)} fusion(f32[32,16,1280]{2,1,0:T(8,128)} %fusion.405, f32[15,16,1280]{2,1,0:T(8,128)} %collective-permute-done.5, f32[15,16,1280]{2,1,0:T(8,128)S(1)} %collective-permute-done.4, f32[]{:T(128)} %bitcast.45, f32[]{:T(128)} %bitcast.44, f32[]{:T(128)} %bitcast.43, f32[]{:T(128)} %bitcast.42, f32[]{:T(128)} %bitcast.41, ...), kind=kLoop, calls=%fused_computation.626 | loop fusion | flops 59637760 | bytes 7700604 | tf_op jit(solution)/shard_map/add | solution.py:30
  183.9 1.3 copy-done.2
  185.5 3.4 collective-permute-start.6
  189.3 2.2 collective-permute-start.7
  191.5 10.0 %collective-permute-done.6 = f32[32,7,1280]{2,0,1:T(8,128)S(1)} collective-permute-done((f32[32,7,1280]{2,0,1:T(8,128)S(1)}, f32[32,7,1280]{2,0,1:T(8,128)S(1)}, u32[]{:S(2)}, u32[]{:S(2)}) %collective-permute-start.6) | collective-permute-done | bytes 1146912 | tf_op jit(solution)/shard_map/ppermute | solution.py:18
  201.5 0.7 copy.21
  202.2 6.1 collective-permute-done.7
  208.3 0.7 copy.23
  209.0 16.4 %fusion.81 = f32[32,16,1280]{2,1,0:T(8,128)S(1)} fusion(f32[32,16,1280]{2,1,0:T(8,128)S(1)} %copy-done, f32[32,16,1280]{2,1,0:T(8,128)S(1)} %copy-done.3, f32[32,7,1280]{2,1,0:T(8,128)S(1)} %copy.23, f32[32,7,1280]{2,1,0:T(8,128)S(1)} %copy.21, f32[]{:T(128)} %bitcast.16, f32[]{:T(128)} %bitcast.15, f32[]{:T(128)} %bitcast.14, f32[]{:T(128)} %bitcast.13, ...), kind=kLoop, calls=%fused_computation.389 | loop fusion | flops 28835840 | bytes 10158140 | tf_op jit(solution)/shard_map/mul | solution.py:53
  226.0 1.9 collective-permute-start.8
  228.3 2.5 collective-permute-start.9
  230.8 9.9 %collective-permute-done.8 = f32[32,7,1280]{2,0,1:T(8,128)S(1)} collective-permute-done((f32[32,7,1280]{2,0,1:T(8,128)S(1)}, f32[32,7,1280]{2,0,1:T(8,128)S(1)}, u32[]{:S(2)}, u32[]{:S(2)}) %collective-permute-start.8) | collective-permute-done | bytes 1146912 | tf_op jit(solution)/shard_map/ppermute | solution.py:18
  240.7 0.7 copy.25
  241.4 5.6 collective-permute-done.9
  247.0 0.7 copy.27
  247.7 17.1 %fusion.42 = f32[32,16,1280]{2,1,0:T(8,128)} fusion(f32[32,16,1280]{2,1,0:T(8,128)S(1)} %fusion.81, f32[32,7,1280]{2,1,0:T(8,128)S(1)} %copy.27, f32[32,7,1280]{2,1,0:T(8,128)S(1)} %copy.25, f32[]{:T(128)} %bitcast.16, f32[]{:T(128)} %bitcast.15, f32[]{:T(128)} %bitcast.14, f32[]{:T(128)} %bitcast.13, f32[]{:T(128)} %bitcast.12, f32[]{:T(128)} %bitcast.11, ...), kind=kLoop, calls=%fused_computation.350 | loop fusion | flops 28180480 | bytes 7536700 | tf_op jit(solution)/shard_map/add | solution.py:30
  264.7 1.8 fusion.511
  266.5 4.6 collective-permute-start.10
  271.1 1.3 collective-permute-start.11
  272.4 12.5 %collective-permute-done.10 = f32[15,16,1280]{2,1,0:T(8,128)S(1)} collective-permute-done((f32[15,16,1280]{2,1,0:T(8,128)S(1)}, f32[15,16,1280]{2,1,0:T(8,128)S(1)}, u32[]{:S(2)}, u32[]{:S(2)}) %collective-permute-start.10) | collective-permute-done | bytes 1228832 | tf_op jit(solution)/shard_map/ppermute | solution.py:18
  284.9 4.3 collective-permute-done.11
  289.2 54.7 %fusion.232 = f32[32,16,1280]{2,1,0:T(8,128)} fusion(f32[32,16,1280]{2,1,0:T(8,128)S(1)} %copy-done, f32[32,16,1280]{2,1,0:T(8,128)} %fusion.42, f32[15,16,1280]{2,1,0:T(8,128)} %collective-permute-done.11, f32[15,16,1280]{2,1,0:T(8,128)S(1)} %collective-permute-done.10, f32[]{:T(128)} %bitcast.45, f32[]{:T(128)} %bitcast.44, f32[]{:T(128)} %bitcast.43, ...), kind=kLoop, calls=%fused_computation.540 | loop fusion | flops 60293120 | bytes 10322044 | tf_op jit(solution)/shard_map/div | solution.py:48
  343.9 1.8 fusion.510
  345.8 3.8 collective-permute-start.12
  349.5 1.5 collective-permute-start.13
  351.0 13.4 %collective-permute-done.12 = f32[15,16,1280]{2,1,0:T(8,128)S(1)} collective-permute-done((f32[15,16,1280]{2,1,0:T(8,128)S(1)}, f32[15,16,1280]{2,1,0:T(8,128)S(1)}, u32[]{:S(2)}, u32[]{:S(2)}) %collective-permute-start.12) | collective-permute-done | bytes 1228832 | tf_op jit(solution)/shard_map/ppermute | solution.py:18
  364.5 4.5 collective-permute-done.13
  368.9 52.2 %fusion.145 = f32[32,16,1280]{2,1,0:T(8,128)S(1)} fusion(f32[32,16,1280]{2,1,0:T(8,128)} %fusion.232, f32[15,16,1280]{2,1,0:T(8,128)} %collective-permute-done.13, f32[15,16,1280]{2,1,0:T(8,128)S(1)} %collective-permute-done.12, f32[]{:T(128)} %bitcast.45, f32[]{:T(128)} %bitcast.44, f32[]{:T(128)} %bitcast.43, f32[]{:T(128)} %bitcast.42, f32[]{:T(128)} %bitcast.41, ...), kind=kLoop, calls=%fused_computation.453 | loop fusion | flops 59637760 | bytes 7700604 | tf_op jit(solution)/shard_map/add | solution.py:30
  421.7 2.3 collective-permute-start.14
  424.4 2.1 collective-permute-start.15
  426.5 10.3 %collective-permute-done.14 = f32[32,7,1280]{2,0,1:T(8,128)S(1)} collective-permute-done((f32[32,7,1280]{2,0,1:T(8,128)S(1)}, f32[32,7,1280]{2,0,1:T(8,128)S(1)}, u32[]{:S(2)}, u32[]{:S(2)}) %collective-permute-start.14) | collective-permute-done | bytes 1146912 | tf_op jit(solution)/shard_map/ppermute | solution.py:18
  436.8 0.7 copy.29
  437.5 5.6 collective-permute-done.15
  443.1 0.7 copy.31
  443.7 17.3 %fusion.507 = (f32[1280]{0:T(1024)S(1)}, f32[32,16,1280]{2,1,0:T(8,128)}) fusion(f32[32,16,1280]{2,1,0:T(8,128)S(1)} %fusion.81, f32[32,7,1280]{2,1,0:T(8,128)S(1)} %copy.31, f32[32,16,1280]{2,1,0:T(8,128)S(1)} %fusion.145, f32[]{:T(128)} %bitcast.3, f32[]{:T(128)} %bitcast.4, f32[]{:T(128)} %bitcast.5, f32[]{:T(128)} %bitcast.6, f32[]{:T(128)} %bitcast.7, ...), kind=kLoop, calls=%fused_computation.845 | loop fusion | flops 29489920 | bytes 10163260 | tf_op jit(solution)/shard_map/reduce_sum | solution.py:56
  461.0 6.7 psum.21
  467.7 65.9 %psum.22 = f32[1280]{0:T(1024)S(1)} all-reduce(f32[1280]{0:T(1024)S(1)} %psum.21), channel_id=1, replica_groups=mesh['rt'=32,'mob'=4] {'rt'}, use_global_device_ids=true, to_apply=%region_2.0 | all-reduce | flops 1280 | bytes 10240 | tf_op jit(solution)/shard_map/psum | solution.py:56
  533.6 1.9 fusion.503
  535.6 1.5 fusion.504
  538.0 91.1 %psum.23 = f32[1280]{0:T(1024)S(1)} all-reduce(f32[1280]{0:T(1024)S(1)} %multiply_reduce_fusion), channel_id=1, replica_groups=mesh['rt'=32,'mob'=4] {'rt','mob'}, use_global_device_ids=true, to_apply=%region_6.0 | all-reduce | flops 1280 | bytes 10240 | tf_op jit(solution)/shard_map/psum | solution.py:60
  629.1 70.0 %reduce-scatter.3.cloned.1.call-done = f32[8,1024]{1,0:T(8,128)} async-done(((f32[256,1024]{1,0:T(8,128)}), f32[8,1024]{1,0:T(8,128)}) %reduce-scatter.3.cloned.1.call-update) | async-done | bytes 32784 | tf_op jit(solution)/shard_map/reduce_scatter | solution.py:67
  699.3 49.3 %reduce-scatter.5.cloned.1.call-done = f32[8,256]{1,0:T(8,128)} async-done(((f32[8,1024]{1,0:T(8,128)}), f32[8,256]{1,0:T(8,128)}) %reduce-scatter.5.cloned.1.call-update) | async-done | bytes 8208 | tf_op jit(solution)/shard_map/reduce_scatter | solution.py:68
  748.6 1.4 multiply_multiply_fusion
  (41 shorter events, 5.8 us)
Async XLA Ops:
  7.2 691.9 %reduce-scatter.3.cloned.1.call-start = ((), (), s32[]{:S(2)}) async-start(), calls=%async_computation.2 | async-start | bytes 1081344 | tf_op jit(solution)/shard_map/reduce_scatter | solution.py:67
  9.1 8.9 %copy-start.6 = (f32[15]{0:T(128)S(1)}, f32[15]{0:T(128)}, u32[]{:S(2)}) copy-start(f32[15]{0:T(128)} %param.7) | copy-start | bytes 184
  9.1 9.6 %copy-start = (f32[32,16,1280]{2,1,0:T(8,128)S(1)}, f32[32,16,1280]{2,1,0:T(8,128)}, u32[]{:S(2)}) copy-start(f32[32,16,1280]{2,1,0:T(8,128)} %param.5) | copy-start | bytes 7864324
  9.5 18.9 %collective-permute-start = (f32[32,7,1280]{2,0,1:T(8,128)S(1)}, f32[32,7,1280]{2,0,1:T(8,128)S(1)}, u32[]{:S(2)}, u32[]{:S(2)}) collective-permute-start(f32[32,7,1280]{2,0,1:T(8,128)S(1)} %copy.32), channel_id=1, source_target_pairs={{0,1},{1,2},{2,3},{4,5},{5,6},{6,7},{8,9},{9,10},{10,11},{12,13},{... | collective-permute-start | bytes 3440648 | tf_op jit(solution)/shard_map/ppermute | solution.py:18
  16.0 18.7 %collective-permute-start.1 = (f32[32,7,1280]{2,0,1:T(8,128)S(1)}, f32[32,7,1280]{2,0,1:T(8,128)S(1)}, u32[]{:S(2)}, u32[]{:S(2)}) collective-permute-start(f32[32,7,1280]{2,0,1:T(8,128)S(1)} %copy.33), channel_id=1, source_target_pairs={{1,0},{2,1},{3,2},{5,4},{6,5},{7,6},{9,8},{10,9},{11,10},{13,12},{... | collective-permute-start | bytes 3440648 | tf_op jit(solution)/shard_map/ppermute | solution.py:20
  50.5 4.8 copy-start.5
  50.6 16.9 %collective-permute-start.2 = (f32[15,16,1280]{2,1,0:T(8,128)S(1)}, f32[15,16,1280]{2,1,0:T(8,128)S(1)}, u32[]{:S(2)}, u32[]{:S(2)}) collective-permute-start(f32[15,16,1280]{2,1,0:T(8,128)S(1)} %get-tuple-element.18), channel_id=1, source_target_pairs={{0,4},{4,8},{8,12},{12,16},{16,20},{20,24},{24,28},{28,32},{32,36}... | collective-permute-start | bytes 3686408 | tf_op jit(solution)/shard_map/ppermute | solution.py:18
  53.9 17.5 %collective-permute-start.3 = (f32[15,16,1280]{2,1,0:T(8,128)S(1)}, f32[15,16,1280]{2,1,0:T(8,128)S(1)}, u32[]{:S(2)}, u32[]{:S(2)}) collective-permute-start(f32[15,16,1280]{2,1,0:T(8,128)S(1)} %get-tuple-element.19), channel_id=1, source_target_pairs={{4,0},{8,4},{12,8},{16,12},{20,16},{24,20},{28,24},{32,28},{36,32}... | collective-permute-start | bytes 3686408 | tf_op jit(solution)/shard_map/ppermute | solution.py:20
  71.4 1.1 copy-start.4
  108.7 17.9 %collective-permute-start.4 = (f32[15,16,1280]{2,1,0:T(8,128)S(1)}, f32[15,16,1280]{2,1,0:T(8,128)S(1)}, u32[]{:S(2)}, u32[]{:S(2)}) collective-permute-start(f32[15,16,1280]{2,1,0:T(8,128)S(1)} %get-tuple-element.16), channel_id=1, source_target_pairs={{0,4},{4,8},{8,12},{12,16},{16,20},{20,24},{24,28},{28,32},{32,36}... | collective-permute-start | bytes 3686408 | tf_op jit(solution)/shard_map/ppermute | solution.py:18
  111.9 18.9 %collective-permute-start.5 = (f32[15,16,1280]{2,1,0:T(8,128)S(1)}, f32[15,16,1280]{2,1,0:T(8,128)}, u32[]{:S(2)}, u32[]{:S(2)}) collective-permute-start(f32[15,16,1280]{2,1,0:T(8,128)S(1)} %get-tuple-element.17), channel_id=1, source_target_pairs={{4,0},{8,4},{12,8},{16,12},{20,16},{24,20},{28,24},{32,28},{36,32}... | collective-permute-start | bytes 3686408 | tf_op jit(solution)/shard_map/ppermute | solution.py:20
  183.7 1.5 copy-start.2
  185.5 16.0 %collective-permute-start.6 = (f32[32,7,1280]{2,0,1:T(8,128)S(1)}, f32[32,7,1280]{2,0,1:T(8,128)S(1)}, u32[]{:S(2)}, u32[]{:S(2)}) collective-permute-start(f32[32,7,1280]{2,0,1:T(8,128)S(1)} %copy.20), channel_id=1, source_target_pairs={{0,1},{1,2},{2,3},{4,5},{5,6},{6,7},{8,9},{9,10},{10,11},{12,13},{... | collective-permute-start | bytes 3440648 | tf_op jit(solution)/shard_map/ppermute | solution.py:18
  189.3 19.6 %copy-start.3 = (f32[32,16,1280]{2,1,0:T(8,128)S(1)}, f32[32,16,1280]{2,1,0:T(8,128)}, u32[]{:S(2)}) copy-start(f32[32,16,1280]{2,1,0:T(8,128)} %copy-done.2) | copy-start | bytes 7864324
  189.3 18.9 %collective-permute-start.7 = (f32[32,7,1280]{2,0,1:T(8,128)S(1)}, f32[32,7,1280]{2,0,1:T(8,128)S(1)}, u32[]{:S(2)}, u32[]{:S(2)}) collective-permute-start(f32[32,7,1280]{2,0,1:T(8,128)S(1)} %copy.22), channel_id=1, source_target_pairs={{1,0},{2,1},{3,2},{5,4},{6,5},{7,6},{9,8},{10,9},{11,10},{13,12},{... | collective-permute-start | bytes 3440648 | tf_op jit(solution)/shard_map/ppermute | solution.py:20
  226.0 14.7 %collective-permute-start.8 = (f32[32,7,1280]{2,0,1:T(8,128)S(1)}, f32[32,7,1280]{2,0,1:T(8,128)S(1)}, u32[]{:S(2)}, u32[]{:S(2)}) collective-permute-start(f32[32,7,1280]{2,0,1:T(8,128)S(1)} %copy.24), channel_id=1, source_target_pairs={{0,1},{1,2},{2,3},{4,5},{5,6},{6,7},{8,9},{9,10},{10,11},{12,13},{... | collective-permute-start | bytes 3440648 | tf_op jit(solution)/shard_map/ppermute | solution.py:18
  228.3 18.7 %collective-permute-start.9 = (f32[32,7,1280]{2,0,1:T(8,128)S(1)}, f32[32,7,1280]{2,0,1:T(8,128)S(1)}, u32[]{:S(2)}, u32[]{:S(2)}) collective-permute-start(f32[32,7,1280]{2,0,1:T(8,128)S(1)} %copy.26), channel_id=1, source_target_pairs={{1,0},{2,1},{3,2},{5,4},{6,5},{7,6},{9,8},{10,9},{11,10},{13,12},{... | collective-permute-start | bytes 3440648 | tf_op jit(solution)/shard_map/ppermute | solution.py:20
  266.5 18.4 %collective-permute-start.10 = (f32[15,16,1280]{2,1,0:T(8,128)S(1)}, f32[15,16,1280]{2,1,0:T(8,128)S(1)}, u32[]{:S(2)}, u32[]{:S(2)}) collective-permute-start(f32[15,16,1280]{2,1,0:T(8,128)S(1)} %get-tuple-element.10), channel_id=1, source_target_pairs={{0,4},{4,8},{8,12},{12,16},{16,20},{20,24},{24,28},{28,32},{32,36}... | collective-permute-start | bytes 3686408 | tf_op jit(solution)/shard_map/ppermute | solution.py:18
  271.1 18.1 %collective-permute-start.11 = (f32[15,16,1280]{2,1,0:T(8,128)S(1)}, f32[15,16,1280]{2,1,0:T(8,128)}, u32[]{:S(2)}, u32[]{:S(2)}) collective-permute-start(f32[15,16,1280]{2,1,0:T(8,128)S(1)} %get-tuple-element.11), channel_id=1, source_target_pairs={{4,0},{8,4},{12,8},{16,12},{20,16},{24,20},{28,24},{32,28},{36,32}... | collective-permute-start | bytes 3686408 | tf_op jit(solution)/shard_map/ppermute | solution.py:20
  345.8 18.7 %collective-permute-start.12 = (f32[15,16,1280]{2,1,0:T(8,128)S(1)}, f32[15,16,1280]{2,1,0:T(8,128)S(1)}, u32[]{:S(2)}, u32[]{:S(2)}) collective-permute-start(f32[15,16,1280]{2,1,0:T(8,128)S(1)} %get-tuple-element.8), channel_id=1, source_target_pairs={{0,4},{4,8},{8,12},{12,16},{16,20},{20,24},{24,28},{28,32},{32,36}... | collective-permute-start | bytes 3686408 | tf_op jit(solution)/shard_map/ppermute | solution.py:18
  349.5 19.4 %collective-permute-start.13 = (f32[15,16,1280]{2,1,0:T(8,128)S(1)}, f32[15,16,1280]{2,1,0:T(8,128)}, u32[]{:S(2)}, u32[]{:S(2)}) collective-permute-start(f32[15,16,1280]{2,1,0:T(8,128)S(1)} %get-tuple-element.9), channel_id=1, source_target_pairs={{4,0},{8,4},{12,8},{16,12},{20,16},{24,20},{28,24},{32,28},{36,32}... | collective-permute-start | bytes 3686408 | tf_op jit(solution)/shard_map/ppermute | solution.py:20
  421.7 15.1 %collective-permute-start.14 = (f32[32,7,1280]{2,0,1:T(8,128)S(1)}, f32[32,7,1280]{2,0,1:T(8,128)S(1)}, u32[]{:S(2)}, u32[]{:S(2)}) collective-permute-start(f32[32,7,1280]{2,0,1:T(8,128)S(1)} %copy.28), channel_id=1, source_target_pairs={{0,1},{1,2},{2,3},{4,5},{5,6},{6,7},{8,9},{9,10},{10,11},{12,13},{... | collective-permute-start | bytes 3440648 | tf_op jit(solution)/shard_map/ppermute | solution.py:18
  424.4 18.7 %collective-permute-start.15 = (f32[32,7,1280]{2,0,1:T(8,128)S(1)}, f32[32,7,1280]{2,0,1:T(8,128)S(1)}, u32[]{:S(2)}, u32[]{:S(2)}) collective-permute-start(f32[32,7,1280]{2,0,1:T(8,128)S(1)} %copy.30), channel_id=1, source_target_pairs={{1,0},{2,1},{3,2},{5,4},{6,5},{7,6},{9,8},{10,9},{11,10},{13,12},{... | collective-permute-start | bytes 3440648 | tf_op jit(solution)/shard_map/ppermute | solution.py:20
  535.5 2.1 copy-start.1
  535.5 213.0 %copy-start.7 = (s32[256]{0:T(256)S(1)}, s32[256]{0:T(256)}, u32[]{:S(2)}) copy-start(s32[256]{0:T(256)} %param.9) | copy-start | bytes 3076
  535.5 213.0 %copy-start.8 = (s32[8]{0:T(128)S(1)}, s32[8]{0:T(128)}, u32[]{:S(2)}) copy-start(s32[8]{0:T(128)} %param.8) | copy-start | bytes 100
  537.0 211.5 %reduce-scatter.5.cloned.1.call-start = ((), (), s32[]{:S(2)}) async-start(), calls=%async_computation.3 | async-start | bytes 40960 | tf_op jit(solution)/shard_map/reduce_scatter | solution.py:68
Sparse Core Ops, SparseCore 0:
  537.2 161.8 reduce-scatter.2
  701.6 46.9 reduce-scatter.4
